TPU v7x, 256 devices: a whole 4x4x8 slice. The times are simulated.
256 devices in a mesh: owner: 16 (over z, core), tensor: 16 (over x, y).
Axes of the slice: x: 4, y: 4, z: 8, core: 2. Of those that a mesh axis runs over, the one named last changes fastest.
Arguments:
- mixer_input: bfloat16 [16384, 2, 8192], P('owner', None, 'tensor'), may hold values from -6 to 6
- step_raw: float32 [16384, 128], P('owner', 'tensor'), may hold values from -7 to 5
- decay_rate: float32 [128], P('tensor'), may hold values from 0.005 to 0.5
- skip_gain: float32 [128], P('tensor'), may hold values from 0.5 to 2
- state_proj: bfloat16 [16384, 2, 4, 256], P('owner'), may hold values from -1.5 to 1.5
- queries: bfloat16 [16384, 4096], P('owner', 'tensor'), may hold values from -256 to 256
- suffix_kv: bfloat16 [16384, 2, 4, 128], P('owner'), may hold values from -6 to 6
- state_pool: bfloat16 [64, 128, 64, 256], P('owner', 'tensor'), may hold values from -1.5 to 1.5
- page_pool: bfloat16 [256, 128, 2, 4, 128], P('owner'), may hold values from -6 to 6
- norm_gain: float32 [8192], P('tensor'), may hold values from 0.1 to 1.9
- hit_owner: int32 [64, 1], replicated, may hold values from 0 to 15; in each aligned block of 4 rows (0 to 3, 4 to 7, ...) at most 2 rows name the same one
- hit_slot: int32 [64], replicated, may hold values from 0 to 3
- page_owner: int32 [64, 16, 1], replicated, may hold values from 0 to 15; in each aligned block of 64 rows (0 to 63, 64 to 127, ..., all dimensions but the last counted through in order) at most 6 rows name the same one
- page_slot: int32 [64, 16], replicated, may hold values from 0 to 15
- prefix_len: int32 [64], replicated, may hold values from 256 to 2048, as said below
- suffix_len: int32 [64], replicated, may hold values from 64 to 256, as said below
Outputs:
- mamba_out: bfloat16 [16384, 8192], P('owner', 'tensor')
- attn_out: bfloat16 [16384, 4096], P('owner', 'tensor')
Inputs may be any that keep to these rules, and one draw needn't show every extreme that they name: `hit_owner`: the 4 requests on one index of owner name one owner at most 2 times, and some index reaches it. `page_owner`: of the 64 list entries of the requests on one index of owner, at most 6 name one owner, and some index reaches it. `prefix_len`: a multiple of 256; request 0 has 2048. `suffix_len`: request 0 has 256.
All inputs are finite; a program needn't handle non-finite values.
Results may differ from a plain program's by a relative error of at most 0.0045.
Values may be sent and summed in bfloat16 or wider, within the bound.
A program may use at most 192 MiB of HBM per device.

v0:
```python
import math
import jax
import jax.numpy as jnp
from jax import lax
from jax.sharding import PartitionSpec as P

SSM_HEAD_TOTAL = 128
MHDIM = 64
STATE = 256
GROUPS = 4
QHEADS = 32
KVHEADS = 4
HD = 128
PAGE = 128
SPAN = 128
SUF = 256
CAP_S = 2
MAXP = 16
EPSILON = 1e-05
NEG_FILL = -1e30


def mixer_core(x_heads, z_heads, rate_raw, decay_groups, skip_groups, b_rows, c_rows, start_state):
    seq_len, group_count, head_count, head_width = x_heads.shape
    blocks = seq_len // SPAN
    step_rate = jax.nn.softplus(rate_raw)
    keep_log = -step_rate * decay_groups[None]
    x_block = x_heads.reshape(blocks, SPAN, group_count, head_count, head_width)
    rate_block = step_rate.reshape(blocks, SPAN, group_count, head_count)
    cum_block = jnp.cumsum(keep_log.reshape(blocks, SPAN, group_count, head_count), axis=1)
    b_block = b_rows.reshape(blocks, SPAN, group_count, -1)
    c_block = c_rows.reshape(blocks, SPAN, group_count, -1)
    intersection = jnp.einsum(
        "cign,cjgn->cgij", c_block, b_block, preferred_element_type=jnp.float32
    )
    cum_moved = jnp.transpose(cum_block, (0, 2, 3, 1))
    rate_moved = jnp.transpose(rate_block, (0, 2, 3, 1))
    lower = jnp.arange(SPAN)[:, None] >= jnp.arange(SPAN)[None, :]
    fade = jnp.exp(jnp.where(lower, cum_moved[..., :, None] - cum_moved[..., None, :], NEG_FILL))
    weights = (intersection[:, :, None] * fade * rate_moved[..., None, :]).astype(jnp.bfloat16)
    inner = jnp.einsum("cghij,cjghp->cighp", weights, x_block, preferred_element_type=jnp.float32)
    cum_end = cum_block[:, -1]
    tail = jnp.exp(cum_end[:, None] - cum_block) * rate_block
    scaled = (tail[..., None] * x_block).astype(jnp.bfloat16)
    block_state = jnp.einsum(
        "cjghp,cjgn->cghpn", scaled, b_block, preferred_element_type=jnp.float32
    )
    carry = start_state.astype(jnp.float32)
    begins = []
    for block_index in range(blocks):
        begins.append(carry)
        carry = jnp.exp(cum_end[block_index])[..., None, None] * carry + block_state[block_index]
    begin_half = jnp.stack(begins).astype(jnp.bfloat16)
    carried = jnp.einsum(
        "cign,cghpn->cighp", c_block, begin_half, preferred_element_type=jnp.float32
    )
    summed = (
        inner
        + jnp.exp(cum_block)[..., None] * carried
        + skip_groups[None, None, :, :, None] * x_block
    )
    gate = jax.nn.silu(z_heads.astype(jnp.float32)).reshape(
        blocks, SPAN, group_count, head_count, head_width
    )
    return (summed * gate).reshape(seq_len, group_count, head_count, head_width)


def attend(query, key_pre, value_pre, key_suf, value_suf, prefix_count):
    softmax_scale = 1.0 / math.sqrt(HD)
    score_pre = (
        jnp.einsum("qhd,md->hqm", query, key_pre, preferred_element_type=jnp.float32)
        * softmax_scale
    )
    score_suf = (
        jnp.einsum("qhd,kd->hqk", query, key_suf, preferred_element_type=jnp.float32)
        * softmax_scale
    )
    pre_live = jnp.arange(key_pre.shape[0]) < prefix_count
    causal = jnp.arange(SUF)[:, None] >= jnp.arange(SUF)[None, :]
    score_pre = jnp.where(pre_live[None, None, :], score_pre, NEG_FILL)
    score_suf = jnp.where(causal[None], score_suf, NEG_FILL)
    row_max = jnp.maximum(jnp.max(score_pre, axis=2), jnp.max(score_suf, axis=2))
    weight_pre = jnp.exp(score_pre - row_max[..., None])
    weight_suf = jnp.exp(score_suf - row_max[..., None])
    denominator = jnp.sum(weight_pre, axis=2) + jnp.sum(weight_suf, axis=2)
    mixed = jnp.einsum(
        "hqm,md->qhd",
        weight_pre.astype(jnp.bfloat16),
        value_pre,
        preferred_element_type=jnp.float32,
    )
    mixed = mixed + jnp.einsum(
        "hqk,kd->qhd",
        weight_suf.astype(jnp.bfloat16),
        value_suf,
        preferred_element_type=jnp.float32,
    )
    return mixed / jnp.transpose(denominator)[:, :, None]


def bucket_plan(owner_rows, live_rows, owner_index, capacity):
    positions = jnp.arange(owner_rows.shape[1])
    matches = (
        (owner_rows[:, :, None] == owner_rows[:, None, :])
        & live_rows[:, None, :]
        & (positions[None, None, :] < positions[None, :, None])
    )
    slot_rank = jnp.sum(matches.astype(jnp.int32), axis=2)
    chosen = (
        (owner_rows[:, None, :] == owner_index)
        & live_rows[:, None, :]
        & (slot_rank[:, None, :] == jnp.arange(capacity)[None, :, None])
    )
    return (slot_rank, chosen)


def bucket_send(table, entry_ids, chosen):
    wanted = jnp.sum(jnp.where(chosen, entry_ids[:, None, :], 0), axis=2).reshape(-1)
    filled = jnp.any(chosen, axis=2).reshape(-1)
    picked = jnp.take(table, wanted, axis=0, mode="clip")
    shaped = jnp.where(
        filled.reshape((-1,) + (1,) * (picked.ndim - 1)), picked, jnp.zeros_like(picked)
    )
    return shaped.reshape(chosen.shape[:2] + picked.shape[1:])


def body(
    mixer_input,
    step_raw,
    decay_rate,
    skip_gain,
    state_proj,
    queries,
    suffix_kv,
    state_pool,
    page_pool,
    norm_gain,
    hit_owner,
    hit_slot,
    page_owner,
    page_slot,
    prefix_len,
    suffix_len,
):
    owners = lax.axis_size("owner")
    owner_index = lax.axis_index("owner")
    column = lax.axis_index("tensor")
    local_count = mixer_input.shape[0] // SUF
    local_heads = decay_rate.shape[0]
    local_qheads = queries.shape[1] // HD
    group_index = column * local_heads // (SSM_HEAD_TOTAL // GROUPS)
    kv_index = column * local_qheads // (QHEADS // KVHEADS)
    first_row = owner_index * local_count
    page_capacity = max(2, (local_count * MAXP + owners - 1) // owners * 3 // 2)
    state_owner = hit_owner[:, 0].reshape(owners, local_count)
    state_slot = hit_slot.reshape(owners, local_count)
    every_live = jnp.ones(state_owner.shape, jnp.bool_)
    state_rank, state_pick = bucket_plan(state_owner, every_live, owner_index, CAP_S)
    outgoing = bucket_send(state_pool, state_slot, state_pick)
    arrived = lax.all_to_all(outgoing, "owner", split_axis=0, concat_axis=0, tiled=True)
    arrived = arrived.reshape((owners * CAP_S,) + arrived.shape[2:])
    local_holder = lax.dynamic_index_in_dim(state_owner, owner_index, 0, keepdims=False)
    my_rank = lax.dynamic_index_in_dim(state_rank, owner_index, 0, keepdims=False)
    start_state = jnp.take(arrived, local_holder * CAP_S + my_rank, axis=0, mode="clip")
    x_heads = mixer_input[:, 0].reshape(local_count, SUF, 1, local_heads, MHDIM)
    z_heads = mixer_input[:, 1].reshape(local_count, SUF, 1, local_heads, MHDIM)
    rate_raw = step_raw.reshape(local_count, SUF, 1, local_heads)
    maps_here = lax.dynamic_index_in_dim(state_proj, group_index, 2, keepdims=True)
    b_rows = maps_here[:, 0].reshape(local_count, SUF, 1, STATE)
    c_rows = maps_here[:, 1].reshape(local_count, SUF, 1, STATE)
    core = jax.vmap(mixer_core, in_axes=(0, 0, 0, None, None, 0, 0, 0))
    gated = core(
        x_heads,
        z_heads,
        rate_raw,
        decay_rate.reshape(1, local_heads),
        skip_gain.reshape(1, local_heads),
        b_rows,
        c_rows,
        start_state.reshape(local_count, 1, local_heads, MHDIM, STATE),
    )
    gated = gated.reshape(local_count * SUF, local_heads * MHDIM)
    partial_sum = jnp.sum(gated * gated, axis=1)
    spread = jnp.where(jnp.arange(GROUPS)[:, None] == group_index, partial_sum[None, :], 0.0)
    totals = lax.psum(spread, "tensor")
    square = lax.dynamic_index_in_dim(totals, group_index, 0, keepdims=False) / (
        SSM_HEAD_TOTAL // GROUPS * MHDIM
    )
    my_suffix = lax.dynamic_slice_in_dim(suffix_len, first_row, local_count, 0)
    active = (jnp.arange(SUF)[None, :] < my_suffix[:, None]).reshape(-1)
    rescaled_input = gated * lax.rsqrt(square + EPSILON)[:, None] * norm_gain[None, :]
    mamba_out = jnp.where(active[:, None], rescaled_input, 0.0).astype(jnp.bfloat16)
    pool_head = lax.dynamic_index_in_dim(page_pool, kv_index, 3, keepdims=False)
    entries = local_count * MAXP
    page_rows = page_owner[:, :, 0].reshape(owners, entries)
    page_ids = page_slot.reshape(owners, entries)
    live_rows = (jnp.arange(MAXP)[None, :] * PAGE < prefix_len[:, None]).reshape(owners, entries)
    my_pages = lax.dynamic_index_in_dim(page_rows, owner_index, 0, keepdims=False)
    my_live = lax.dynamic_index_in_dim(live_rows, owner_index, 0, keepdims=False)
    page_rank, page_pick = bucket_plan(page_rows, live_rows, owner_index, page_capacity)
    sending = bucket_send(pool_head, page_ids, page_pick)
    received_rows = lax.all_to_all(sending, "owner", split_axis=0, concat_axis=0, tiled=True)
    received_rows = received_rows.reshape((owners * page_capacity,) + received_rows.shape[2:])
    my_page_rank = lax.dynamic_index_in_dim(page_rank, owner_index, 0, keepdims=False)
    fetched = jnp.take(received_rows, my_pages * page_capacity + my_page_rank, axis=0, mode="clip")
    fetched = jnp.where(my_live[:, None, None, None], fetched, jnp.zeros_like(fetched))
    prefix_kv = fetched.reshape(local_count, MAXP * PAGE, 2, HD)
    my_prefix = lax.dynamic_slice_in_dim(prefix_len, first_row, local_count, 0)
    owned_key_value = lax.dynamic_index_in_dim(suffix_kv, kv_index, 2, keepdims=False).reshape(
        local_count, SUF, 2, HD
    )
    query = queries.reshape(local_count, SUF, local_qheads, HD)
    mixed = jax.vmap(attend)(
        query,
        prefix_kv[:, :, 0],
        prefix_kv[:, :, 1],
        owned_key_value[:, :, 0],
        owned_key_value[:, :, 1],
        my_prefix,
    )
    attn_rows = mixed.reshape(local_count * SUF, local_qheads * HD)
    attn_out = jnp.where(active[:, None], attn_rows, 0.0).astype(jnp.bfloat16)
    return (mamba_out, attn_out)


def solution(mesh):
    return jax.shard_map(
        body,
        mesh=mesh,
        in_specs=(
            P("owner", None, "tensor"),
            P("owner", "tensor"),
            P("tensor"),
            P("tensor"),
            P("owner", None, None, None),
            P("owner", "tensor"),
            P("owner", None, None, None),
            P("owner", "tensor", None, None),
            P("owner", None, None, None, None),
            P("tensor"),
            P(),
            P(),
            P(),
            P(),
            P(),
            P(),
        ),
        out_specs=(P("owner", "tensor"), P("owner", "tensor")),
        check_vma=False,
    )
```

profile of v0, /device:TPU:96, one launch (start us, length us, event | category | flops | bytes accessed | tf_op | source)
XLA Modules:
  0.0 448.7 jit_solution(13598574537655978479)
XLA Ops:
  2.7 4.6 %constant_dynamic-slice_fusion.4 = bf16[16,128,2,1,128]{4,3,2,1,0:T(2,128)(2,1)S(1)} fusion(bf16[16,128,2,4,128]{4,3,2,1,0:T(4,128)(2,1)} %param.24, s32[]{:T(128)S(6)} %select_n.125), kind=kLoop, calls=%fused_computation.95 | loop fusion | bytes 2097156 | tf_op jit(solution)/shard_map/jit(dynamic_index_in_dim)/dynamic_slice | solution.py:193
  9.4 6.0 %gather_fusion.2 = bf16[96,128,2,128]{3,1,2,0:T(8,128)(2,1)} fusion(bf16[16,128,2,128]{3,1,2,0:T(8,128)(2,1)S(1)} %bitcast.137, s32[1024]{0:T(1024)S(1)} %pad_clamp_fusion.1), kind=kCustom, calls=%fused_computation.2 | custom fusion | bytes 12583296 | tf_op jit(solution)/shard_map/jit(_take)/gather | solution.py:120
  15.4 5.9 %broadcast_select_fusion.1 = bf16[16,6,128,2,128]{4,2,3,1,0:T(8,128)(2,1)} fusion(bf16[16,6,128,2,128]{4,2,3,1,0:T(8,128)(2,1)} %bitcast.139, pred[16,6]{1,0:T(8,128)(4,1)S(1)} %copy.187), kind=kLoop, calls=%fused_computation.13 | loop fusion | flops 3145728 | bytes 12583008 | tf_op jit(solution)/shard_map/jit(_where)/select_n | solution.py:121
  21.3 7.8 %all-to-all-start.1 = ((bf16[16,6,128,2,128]{4,2,3,1,0:T(8,128)(2,1)}), bf16[16,6,128,2,128]{4,2,3,1,0:T(8,128)(2,1)}, u32[]{:S(2)}, u32[]{:S(2)}) async-start(bf16[16,6,128,2,128]{4,2,3,1,0:T(8,128)(2,1)} %broadcast_select_fusion.1), calls=%async_computation.1 | async-start | bytes 12582912 | tf_op jit(solution)/shard_map/all_to_all | solution.py:202
  31.2 4.8 %gather_fusion = bf16[32,8,64,256]{3,2,1,0:T(8,128)(2,1)} fusion(bf16[4,8,64,256]{3,2,1,0:T(8,128)(2,1)S(1)} %copy-done.2, s32[1024]{0:T(1024)S(1)} %pad_clamp_fusion.3), kind=kCustom, calls=%fused_computation | custom fusion | bytes 16777344 | tf_op jit(solution)/shard_map/jit(_take)/gather | solution.py:120
  36.0 7.2 %broadcast_select_fusion = bf16[16,2,8,64,256]{4,3,2,1,0:T(8,128)(2,1)} fusion(bf16[16,2,8,64,256]{4,3,2,1,0:T(8,128)(2,1)} %bitcast.138, pred[16,2]{1,0:T(8,128)(4,1)S(1)} %copy.171), kind=kLoop, calls=%fused_computation.12 | loop fusion | flops 4194304 | bytes 16777248 | tf_op jit(solution)/shard_map/jit(_where)/select_n | solution.py:121
  43.2 124.6 %all-to-all-done.1 = bf16[16,6,128,2,128]{4,2,3,1,0:T(8,128)(2,1)} async-done(((bf16[16,6,128,2,128]{4,2,3,1,0:T(8,128)(2,1)}), bf16[16,6,128,2,128]{4,2,3,1,0:T(8,128)(2,1)}, u32[]{:S(2)}, u32[]{:S(2)}) %all-to-all-start.1) | async-done | bytes 6291488 | tf_op jit(solution)/shard_map/all_to_all | solution.py:202
  167.8 5.3 %all-to-all-start = ((bf16[16,2,8,64,256]{4,3,2,1,0:T(8,128)(2,1)}), bf16[16,2,8,64,256]{4,3,2,1,0:T(8,128)(2,1)}, u32[]{:S(2)}, u32[]{:S(2)}) async-start(bf16[16,2,8,64,256]{4,3,2,1,0:T(8,128)(2,1)} %broadcast_select_fusion), calls=%async_computation | async-start | bytes 16777216 | tf_op jit(solution)/shard_map/all_to_all | solution.py:160
  173.1 6.9 %fusion.50 = (bf16[1024,1,512]{2,1,0:T(2,128)(2,1)}, bf16[1024,1,512]{2,1,0:T(2,128)(2,1)}) fusion(bf16[1024,2,512]{2,1,0:T(2,128)(2,1)} %param.16), kind=kLoop, calls=%fused_computation.115 | loop fusion | bytes 4194304 | tf_op jit(solution)/shard_map/slice | solution.py:166
  180.1 5.8 %copy.165 = bf16[1024,1,512]{0,2,1:T(8,128)(2,1)} copy(bf16[1024,1,512]{2,1,0:T(2,128)(2,1)} %get-tuple-element.15) | data formatting | bytes 2097152 | tf_op jit(solution)/shard_map/slice | solution.py:165
  185.9 4.7 %copy_convert_fusion = (f32[1024,1,512]{2,0,1:T(8,128)}, f32[1024,1,512]{2,0,1:T(8,128)}) fusion(bf16[1024,1,512]{2,1,0:T(2,128)(2,1)} %get-tuple-element.14, bf16[1024,1,512]{2,1,0:T(2,128)(2,1)} %get-tuple-element.15), kind=kLoop, calls=%fused_computation.52 | loop fusion | flops 1048576 | bytes 6291456 | tf_op jit(solution)/shard_map/vmap()/convert_element_type | solution.py:62
  190.7 6.1 %copy.182 = f32[1024,1,512]{0,1,2:T(1,128)} copy(f32[1024,1,512]{2,0,1:T(8,128)} %get-tuple-element.26) | data formatting | bytes 4194304 | tf_op jit(solution)/shard_map/vmap()/convert_element_type | solution.py:62
  196.8 6.1 %copy.179 = f32[1024,1,512]{0,1,2:T(1,128)} copy(f32[1024,1,512]{2,0,1:T(8,128)} %get-tuple-element.27) | data formatting | bytes 4194304 | tf_op jit(solution)/shard_map/vmap()/convert_element_type | solution.py:44
  202.9 5.4 %constant_dynamic-slice_fusion.8 = (bf16[1024,1,1,256]{3,2,1,0:T(2,128)(2,1)}, bf16[1024,1,1,256]{3,2,1,0:T(2,128)(2,1)S(1)}) fusion(bf16[1024,2,4,256]{3,2,1,0:T(4,128)(2,1)} %param.20, s32[]{:T(128)S(6)} %select_n.115, s32[]{:T(128)S(6)} %add.163), kind=kLoop, calls=%fused_computation.99 | loop fusion | bytes 2097160 | tf_op jit(solution)/shard_map/slice | solution.py:169
  225.6 2.7 convolution_bitcast_fusion
  229.1 3.3 fusion.6
  232.5 5.9 %gather_fusion.3 = bf16[64,128,2,128]{3,1,2,0:T(8,128)(2,1)} fusion(bf16[96,128,2,128]{3,1,2,0:T(8,128)(2,1)} %bitcast.33, s32[1024]{0:T(1024)S(1)} %pad_clamp_fusion), kind=kCustom, calls=%fused_computation.3 | custom fusion | bytes 8388864 | tf_op jit(solution)/shard_map/jit(_take)/gather | solution.py:205
  243.1 3.2 bitcast_reduce_fusion
  246.6 4.5 %fusion.1 = f32[4,2,256]{2,1,0:T(2,128)S(1)} fusion(f32[4,2048,256,2]{2,1,3,0:T(8,128)S(1)} %get-tuple-element.23, f32[4,2,256]{2,1,0:T(2,128)S(1)} %max.43, pred[4,2048]{1,0:T(4,128)(4,1)S(1)} %iota_compare_fusion.3), kind=kLoop, calls=%fused_computation.8 | loop fusion | flops 16775168 | bytes 16801792 | tf_op jit(solution)/shard_map/vmap()/reduce_sum | solution.py:85
  251.2 4.7 %fusion.3 = f32[4,128,2,256]{3,1,2,0:T(8,128)S(1)} fusion(f32[4,2048,256,2]{2,1,3,0:T(8,128)S(1)} %get-tuple-element.23, f32[4,2,256]{2,1,0:T(2,128)S(1)} %max.43, pred[4,2048]{1,0:T(4,128)(4,1)S(1)} %iota_compare_fusion.3, bf16[4,2048,2,128]{3,1,0,2:T(8,128)(2,1)S(1)} %bitcast_select_fusion), kind=kOutput, calls=%fused_computation.10 | convolution fusion | flops 1090519040 | bytes 19939328 | tf_op jit(solution)/shard_map/vmap(hqm,md->qhd)/dot_general | solution.py:86
  259.5 97.2 %all-to-all-done = bf16[16,2,8,64,256]{4,3,2,1,0:T(8,128)(2,1)} async-done(((bf16[16,2,8,64,256]{4,3,2,1,0:T(8,128)(2,1)}), bf16[16,2,8,64,256]{4,3,2,1,0:T(8,128)(2,1)}, u32[]{:S(2)}, u32[]{:S(2)}) %all-to-all-start) | async-done | bytes 8388640 | tf_op jit(solution)/shard_map/all_to_all | solution.py:160
  356.8 4.0 gather_fusion.1
  367.8 2.7 reshape.582
  370.7 74.6 %psum.7 = f32[4,1024]{1,0:T(4,128)S(1)} all-reduce(f32[4,1024]{1,0:T(4,128)S(1)} %broadcast_select_fusion.2), channel_id=1, replica_groups=mesh['owner'=16,'tensor'=16] {'tensor'}, use_global_device_ids=true, to_apply=%region_5.6 | all-reduce | flops 4096 | bytes 32768 | tf_op jit(solution)/shard_map/psum | solution.py:185
  (124 shorter events, 43.2 us)
Async XLA Ops:
  0.6 222.6 %copy-start = (bf16[1024,2,4,128]{3,2,1,0:T(4,128)(2,1)S(1)}, bf16[1024,2,4,128]{3,2,1,0:T(4,128)(2,1)}, u32[]{:S(2)}) copy-start(bf16[1024,2,4,128]{3,2,1,0:T(4,128)(2,1)} %param.22) | copy-start | bytes 6291460
  7.3 0.7 copy-start.11
  21.3 7.8 %copy-start.14 = (s32[64]{0:T(128)S(1)}, s32[64]{0:T(128)}, u32[]{:S(2)}) copy-start(s32[64]{0:T(128)} %param.27) | copy-start | bytes 772
  21.3 8.5 %copy-start.16 = (s32[64,1]{0,1:T(1,128)S(1)}, s32[64,1]{0,1:T(1,128)}, u32[]{:S(2)}) copy-start(s32[64,1]{0,1:T(1,128)} %param.26) | copy-start | bytes 772
  21.3 9.9 %copy-start.2 = (bf16[4,8,64,256]{3,2,1,0:T(8,128)(2,1)S(1)}, bf16[4,8,64,256]{3,2,1,0:T(8,128)(2,1)}, u32[]{:S(2)}) copy-start(bf16[4,8,64,256]{3,2,1,0:T(8,128)(2,1)} %param.23) | copy-start | bytes 3145732
  21.3 146.5 %all-to-all-start.1 = ((bf16[16,6,128,2,128]{4,2,3,1,0:T(8,128)(2,1)}), bf16[16,6,128,2,128]{4,2,3,1,0:T(8,128)(2,1)}, u32[]{:S(2)}, u32[]{:S(2)}) async-start(bf16[16,6,128,2,128]{4,2,3,1,0:T(8,128)(2,1)} %broadcast_select_fusion.1), calls=%async_computation.1 | async-start | bytes 12582912 | tf_op jit(solution)/shard_map/all_to_all | solution.py:202
  167.8 189.0 %all-to-all-start = ((bf16[16,2,8,64,256]{4,3,2,1,0:T(8,128)(2,1)}), bf16[16,2,8,64,256]{4,3,2,1,0:T(8,128)(2,1)}, u32[]{:S(2)}, u32[]{:S(2)}) async-start(bf16[16,2,8,64,256]{4,3,2,1,0:T(8,128)(2,1)} %broadcast_select_fusion), calls=%async_computation | async-start | bytes 16777216 | tf_op jit(solution)/shard_map/all_to_all | solution.py:160
  202.9 5.5 %copy-start.10 = (f32[1024,8]{0,1:T(8,128)S(1)}, f32[1024,8]{0,1:T(8,128)}, u32[]{:S(2)}) copy-start(f32[1024,8]{0,1:T(8,128)} %param.17) | copy-start | bytes 98308
  208.2 1.1 copy-start.13
  215.6 5.1 %copy-start.15 = (s32[64]{0:T(128)S(1)}, s32[64]{0:T(128)}, u32[]{:S(2)}) copy-start(s32[64]{0:T(128)} %param.30) | copy-start | bytes 772
  215.6 5.2 %copy-start.17 = (s32[64]{0:T(128)S(1)}, s32[64]{0:T(128)}, u32[]{:S(2)}) copy-start(s32[64]{0:T(128)} %param.31) | copy-start | bytes 772
  223.1 1.6 copy-start.3
  224.4 4.2 copy-start.6
  225.5 3.1 copy-start.8
  241.0 2.1 copy-start.9
  251.2 4.8 %copy-start.7 = (bf16[1024,2,1,128]{3,0,1,2:T(8,128)(2,1)S(1)}, bf16[1024,2,1,128]{3,0,1,2:T(8,128)(2,1)}, u32[]{:S(2)}) copy-start(bf16[1024,2,1,128]{3,0,1,2:T(8,128)(2,1)} %copy-done.6) | copy-start | bytes 1572868
  360.8 2.2 copy-start.4
  360.8 2.8 copy-start.5
  360.8 2.8 copy-start.18
  367.8 77.5 %copy-start.12 = (f32[512]{0:T(512)S(1)}, f32[512]{0:T(512)}, u32[]{:S(2)}) copy-start(f32[512]{0:T(512)} %param.25) | copy-start | bytes 6148
  445.3 3.4 copy-start.1
where the time goes:
time: 450 us; the launch traced here: 449 us
  waiting for transfers between devices  222 us (49%)
  local copies, waits for them, and re-layouts  82.6 us (18%)
  blocking collectives  74.6 us (17%)
  other arithmetic  36.9 us (8%)
  matrix products  18.6 us (4%)
  starting transfers between devices  13.1 us (3%)
    all_to_all x1, waiting for transfers between devices, body(): lax.all_to_all(sending, 'owner', split_axis=0, concat_axis=0, tiled=True)  125 us
    all_to_all x1, waiting for transfers between devices, body(): lax.all_to_all(outgoing, 'owner', split_axis=0, concat_axis=0, tiled=True)  97.2 us
    psum x1, blocking collectives, body(): totals = lax.psum(spread, 'tensor')  74.6 us
    select_n x2, other arithmetic, bucket_send(): jnp.where(filled.reshape((-1,) + (1,) * (picked.ndim - 1)), picked, jnp.z...  13.1 us
    gather x2, local copies, waits for them, and re-layouts, bucket_send(): picked = jnp.take(table, wanted, axis=0, mode='clip')  10.8 us
  transfers between devices with their start and end apart: 2, of which 2 were waited for; matrix products, arithmetic and copies ran while one was open for 22% of the time, Pallas kernels for 0%

commit v1 on v0

--- a/solution.py
+++ b/solution.py
@@ -182,7 +182,7 @@
     gated = gated.reshape(local_count * SUF, local_heads * MHDIM)
     partial_sum = jnp.sum(gated * gated, axis=1)
     spread = jnp.where(jnp.arange(GROUPS)[:, None] == group_index, partial_sum[None, :], 0.0)
-    totals = lax.psum(spread, "tensor")
+    totals = jnp.sum(lax.all_gather(spread, "tensor"), axis=0)
     square = lax.dynamic_index_in_dim(totals, group_index, 0, keepdims=False) / (
         SSM_HEAD_TOTAL // GROUPS * MHDIM
     )

time: 450 us -> 401 us (0.89)
  blocking collectives: 74.6 us -> 24 us
    psum x1 -> x0, blocking collectives: 74.6 us -> none  [body(): totals = lax.psum(spread, 'tensor')]
    all_gather x0 -> x1, blocking collectives: none -> 24 us  [body(): totals = jnp.sum(lax.all_gather(spread, 'tensor'), axis=0)]
  transfers between devices with their start and end apart: 2 -> 2, of which waited for: 2 -> 2; matrix products, arithmetic and copies ran while one was open for 22% -> 25% of each run, Pallas kernels for 0% -> 0%
where the time goes in v1:
time: 401 us; the launch traced here: 398 us
  waiting for transfers between devices  222 us (55%)
  local copies, waits for them, and re-layouts  82.6 us (21%)
  other arithmetic  36.9 us (9%)
  blocking collectives  24 us (6%)
  matrix products  18.6 us (5%)
  starting transfers between devices  13.1 us (3%)
    all_to_all x1, waiting for transfers between devices, body(): lax.all_to_all(sending, 'owner', split_axis=0, concat_axis=0, tiled=True)  125 us
    all_to_all x1, waiting for transfers between devices, body(): lax.all_to_all(outgoing, 'owner', split_axis=0, concat_axis=0, tiled=True)  97.2 us
    all_gather x1, blocking collectives, body(): totals = jnp.sum(lax.all_gather(spread, 'tensor'), axis=0)  24 us
    select_n x2, other arithmetic, bucket_send(): jnp.where(filled.reshape((-1,) + (1,) * (picked.ndim - 1)), picked, jnp.z...  13.1 us
    gather x2, local copies, waits for them, and re-layouts, bucket_send(): picked = jnp.take(table, wanted, axis=0, mode='clip')  10.8 us
    gather x2, local copies, waits for them, and re-layouts, body(): jnp.take(received_rows, my_pages * page_capacity + my_page_rank, axis=0,...  8.44 us
  transfers between devices with their start and end apart: 2, of which 2 were waited for; matrix products, arithmetic and copies ran while one was open for 25% of the time, Pallas kernels for 0%

profile of v1, /device:TPU:96, one launch (start us, length us, event | category | flops | bytes accessed | tf_op | source)
XLA Modules:
  0.0 398.2 jit_solution(8240992500025776710)
XLA Ops:
  2.7 4.6 %constant_dynamic-slice_fusion.4 = bf16[16,128,2,1,128]{4,3,2,1,0:T(2,128)(2,1)S(1)} fusion(bf16[16,128,2,4,128]{4,3,2,1,0:T(4,128)(2,1)} %param.24, s32[]{:T(128)S(6)} %select_n.132), kind=kLoop, calls=%fused_computation.95 | loop fusion | bytes 2097156 | tf_op jit(solution)/shard_map/jit(dynamic_index_in_dim)/dynamic_slice | solution.py:193
  9.4 6.0 %gather_fusion.2 = bf16[96,128,2,128]{3,1,2,0:T(8,128)(2,1)} fusion(bf16[16,128,2,128]{3,1,2,0:T(8,128)(2,1)S(1)} %bitcast.137, s32[1024]{0:T(1024)S(1)} %pad_clamp_fusion.1), kind=kCustom, calls=%fused_computation.2 | custom fusion | bytes 12583296 | tf_op jit(solution)/shard_map/jit(_take)/gather | solution.py:120
  15.4 5.9 %broadcast_select_fusion.1 = bf16[16,6,128,2,128]{4,2,3,1,0:T(8,128)(2,1)} fusion(bf16[16,6,128,2,128]{4,2,3,1,0:T(8,128)(2,1)} %bitcast.139, pred[16,6]{1,0:T(8,128)(4,1)S(1)} %copy.222), kind=kLoop, calls=%fused_computation.13 | loop fusion | flops 3145728 | bytes 12583008 | tf_op jit(solution)/shard_map/jit(_where)/select_n | solution.py:121
  21.3 7.8 %all-to-all-start.1 = ((bf16[16,6,128,2,128]{4,2,3,1,0:T(8,128)(2,1)}), bf16[16,6,128,2,128]{4,2,3,1,0:T(8,128)(2,1)}, u32[]{:S(2)}, u32[]{:S(2)}) async-start(bf16[16,6,128,2,128]{4,2,3,1,0:T(8,128)(2,1)} %broadcast_select_fusion.1), calls=%async_computation.1 | async-start | bytes 12582912 | tf_op jit(solution)/shard_map/all_to_all | solution.py:202
  31.2 4.8 %gather_fusion = bf16[32,8,64,256]{3,2,1,0:T(8,128)(2,1)} fusion(bf16[4,8,64,256]{3,2,1,0:T(8,128)(2,1)S(1)} %copy-done.2, s32[1024]{0:T(1024)S(1)} %pad_clamp_fusion.3), kind=kCustom, calls=%fused_computation | custom fusion | bytes 16777344 | tf_op jit(solution)/shard_map/jit(_take)/gather | solution.py:120
  36.0 7.2 %broadcast_select_fusion = bf16[16,2,8,64,256]{4,3,2,1,0:T(8,128)(2,1)} fusion(bf16[16,2,8,64,256]{4,3,2,1,0:T(8,128)(2,1)} %bitcast.138, pred[16,2]{1,0:T(8,128)(4,1)S(1)} %copy.206), kind=kLoop, calls=%fused_computation.12 | loop fusion | flops 4194304 | bytes 16777248 | tf_op jit(solution)/shard_map/jit(_where)/select_n | solution.py:121
  43.2 124.6 %all-to-all-done.1 = bf16[16,6,128,2,128]{4,2,3,1,0:T(8,128)(2,1)} async-done(((bf16[16,6,128,2,128]{4,2,3,1,0:T(8,128)(2,1)}), bf16[16,6,128,2,128]{4,2,3,1,0:T(8,128)(2,1)}, u32[]{:S(2)}, u32[]{:S(2)}) %all-to-all-start.1) | async-done | bytes 6291488 | tf_op jit(solution)/shard_map/all_to_all | solution.py:202
  167.8 5.3 %all-to-all-start = ((bf16[16,2,8,64,256]{4,3,2,1,0:T(8,128)(2,1)}), bf16[16,2,8,64,256]{4,3,2,1,0:T(8,128)(2,1)}, u32[]{:S(2)}, u32[]{:S(2)}) async-start(bf16[16,2,8,64,256]{4,3,2,1,0:T(8,128)(2,1)} %broadcast_select_fusion), calls=%async_computation | async-start | bytes 16777216 | tf_op jit(solution)/shard_map/all_to_all | solution.py:160
  173.1 6.9 %fusion.50 = (bf16[1024,1,512]{2,1,0:T(2,128)(2,1)}, bf16[1024,1,512]{2,1,0:T(2,128)(2,1)}) fusion(bf16[1024,2,512]{2,1,0:T(2,128)(2,1)} %param.16), kind=kLoop, calls=%fused_computation.115 | loop fusion | bytes 4194304 | tf_op jit(solution)/shard_map/slice | solution.py:166
  180.1 5.8 %copy.200 = bf16[1024,1,512]{0,2,1:T(8,128)(2,1)} copy(bf16[1024,1,512]{2,1,0:T(2,128)(2,1)} %get-tuple-element.17) | data formatting | bytes 2097152 | tf_op jit(solution)/shard_map/slice | solution.py:165
  185.9 4.7 %copy_convert_fusion = (f32[1024,1,512]{2,0,1:T(8,128)}, f32[1024,1,512]{2,0,1:T(8,128)}) fusion(bf16[1024,1,512]{2,1,0:T(2,128)(2,1)} %get-tuple-element.16, bf16[1024,1,512]{2,1,0:T(2,128)(2,1)} %get-tuple-element.17), kind=kLoop, calls=%fused_computation.52 | loop fusion | flops 1048576 | bytes 6291456 | tf_op jit(solution)/shard_map/vmap()/convert_element_type | solution.py:62
  190.7 6.1 %copy.217 = f32[1024,1,512]{0,1,2:T(1,128)} copy(f32[1024,1,512]{2,0,1:T(8,128)} %get-tuple-element.28) | data formatting | bytes 4194304 | tf_op jit(solution)/shard_map/vmap()/convert_element_type | solution.py:62
  196.8 6.1 %copy.214 = f32[1024,1,512]{0,1,2:T(1,128)} copy(f32[1024,1,512]{2,0,1:T(8,128)} %get-tuple-element.29) | data formatting | bytes 4194304 | tf_op jit(solution)/shard_map/vmap()/convert_element_type | solution.py:44
  202.9 5.4 %constant_dynamic-slice_fusion.8 = (bf16[1024,1,1,256]{3,2,1,0:T(2,128)(2,1)}, bf16[1024,1,1,256]{3,2,1,0:T(2,128)(2,1)S(1)}) fusion(bf16[1024,2,4,256]{3,2,1,0:T(4,128)(2,1)} %param.20, s32[]{:T(128)S(6)} %select_n.122, s32[]{:T(128)S(6)} %add.161), kind=kLoop, calls=%fused_computation.99 | loop fusion | bytes 2097160 | tf_op jit(solution)/shard_map/slice | solution.py:169
  225.6 2.7 convolution_bitcast_fusion
  229.1 3.3 fusion.6
  232.5 5.9 %gather_fusion.3 = bf16[64,128,2,128]{3,1,2,0:T(8,128)(2,1)} fusion(bf16[96,128,2,128]{3,1,2,0:T(8,128)(2,1)} %bitcast.33, s32[1024]{0:T(1024)S(1)} %pad_clamp_fusion), kind=kCustom, calls=%fused_computation.3 | custom fusion | bytes 8388864 | tf_op jit(solution)/shard_map/jit(_take)/gather | solution.py:205
  243.1 3.2 bitcast_reduce_fusion
  246.6 4.5 %fusion.1 = f32[4,2,256]{2,1,0:T(2,128)S(1)} fusion(f32[4,2048,256,2]{2,1,3,0:T(8,128)S(1)} %get-tuple-element.25, f32[4,2,256]{2,1,0:T(2,128)S(1)} %max.43, pred[4,2048]{1,0:T(4,128)(4,1)S(1)} %iota_compare_fusion.3), kind=kLoop, calls=%fused_computation.8 | loop fusion | flops 16775168 | bytes 16801792 | tf_op jit(solution)/shard_map/vmap()/reduce_sum | solution.py:85
  251.2 4.7 %fusion.3 = f32[4,128,2,256]{3,1,2,0:T(8,128)S(1)} fusion(f32[4,2048,256,2]{2,1,3,0:T(8,128)S(1)} %get-tuple-element.25, f32[4,2,256]{2,1,0:T(2,128)S(1)} %max.43, pred[4,2048]{1,0:T(4,128)(4,1)S(1)} %iota_compare_fusion.3, bf16[4,2048,2,128]{3,1,0,2:T(8,128)(2,1)S(1)} %bitcast_select_fusion), kind=kOutput, calls=%fused_computation.10 | convolution fusion | flops 1090519040 | bytes 19939328 | tf_op jit(solution)/shard_map/vmap(hqm,md->qhd)/dot_general | solution.py:86
  259.5 97.2 %all-to-all-done = bf16[16,2,8,64,256]{4,3,2,1,0:T(8,128)(2,1)} async-done(((bf16[16,2,8,64,256]{4,3,2,1,0:T(8,128)(2,1)}), bf16[16,2,8,64,256]{4,3,2,1,0:T(8,128)(2,1)}, u32[]{:S(2)}, u32[]{:S(2)}) %all-to-all-start) | async-done | bytes 8388640 | tf_op jit(solution)/shard_map/all_to_all | solution.py:160
  356.8 4.0 %gather_fusion.1 = bf16[4,8,64,256]{3,2,1,0:T(8,128)(2,1)S(1)} fusion(bf16[32,8,64,256]{3,2,1,0:T(8,128)(2,1)} %bitcast.13, s32[1024]{0:T(1024)S(1)} %pad_clamp_fusion.2), kind=kCustom, calls=%fused_computation.1 | custom fusion | bytes 2097168 | tf_op jit(solution)/shard_map/jit(_take)/gather | solution.py:164
  367.8 2.7 reshape.628
  370.7 24.0 %all_gather.4 = f32[16,4,1024]{2,1,0:T(4,128)S(1)} all-gather(f32[1,4,1024]{2,1,0:T(4,128)S(1)} %broadcast_select_fusion.2), channel_id=1, replica_groups=mesh['owner'=16,'tensor'=16] {'tensor'}, dimensions={0}, use_global_device_ids=true | all-gather | bytes 278528 | tf_op jit(solution)/shard_map/all_gather | solution.py:185
  (125 shorter events, 43.2 us)
Async XLA Ops:
  0.6 222.6 %copy-start = (bf16[1024,2,4,128]{3,2,1,0:T(4,128)(2,1)S(1)}, bf16[1024,2,4,128]{3,2,1,0:T(4,128)(2,1)}, u32[]{:S(2)}) copy-start(bf16[1024,2,4,128]{3,2,1,0:T(4,128)(2,1)} %param.22) | copy-start | bytes 6291460
  7.3 0.7 copy-start.11
  21.3 7.8 %copy-start.14 = (s32[64]{0:T(128)S(1)}, s32[64]{0:T(128)}, u32[]{:S(2)}) copy-start(s32[64]{0:T(128)} %param.27) | copy-start | bytes 772
  21.3 8.5 %copy-start.16 = (s32[64,1]{0,1:T(1,128)S(1)}, s32[64,1]{0,1:T(1,128)}, u32[]{:S(2)}) copy-start(s32[64,1]{0,1:T(1,128)} %param.26) | copy-start | bytes 772
  21.3 9.9 %copy-start.2 = (bf16[4,8,64,256]{3,2,1,0:T(8,128)(2,1)S(1)}, bf16[4,8,64,256]{3,2,1,0:T(8,128)(2,1)}, u32[]{:S(2)}) copy-start(bf16[4,8,64,256]{3,2,1,0:T(8,128)(2,1)} %param.23) | copy-start | bytes 3145732
  21.3 146.5 %all-to-all-start.1 = ((bf16[16,6,128,2,128]{4,2,3,1,0:T(8,128)(2,1)}), bf16[16,6,128,2,128]{4,2,3,1,0:T(8,128)(2,1)}, u32[]{:S(2)}, u32[]{:S(2)}) async-start(bf16[16,6,128,2,128]{4,2,3,1,0:T(8,128)(2,1)} %broadcast_select_fusion.1), calls=%async_computation.1 | async-start | bytes 12582912 | tf_op jit(solution)/shard_map/all_to_all | solution.py:202
  167.8 189.0 %all-to-all-start = ((bf16[16,2,8,64,256]{4,3,2,1,0:T(8,128)(2,1)}), bf16[16,2,8,64,256]{4,3,2,1,0:T(8,128)(2,1)}, u32[]{:S(2)}, u32[]{:S(2)}) async-start(bf16[16,2,8,64,256]{4,3,2,1,0:T(8,128)(2,1)} %broadcast_select_fusion), calls=%async_computation | async-start | bytes 16777216 | tf_op jit(solution)/shard_map/all_to_all | solution.py:160
  202.9 5.5 %copy-start.10 = (f32[1024,8]{0,1:T(8,128)S(1)}, f32[1024,8]{0,1:T(8,128)}, u32[]{:S(2)}) copy-start(f32[1024,8]{0,1:T(8,128)} %param.17) | copy-start | bytes 98308
  208.2 1.1 copy-start.13
  215.6 5.1 %copy-start.15 = (s32[64]{0:T(128)S(1)}, s32[64]{0:T(128)}, u32[]{:S(2)}) copy-start(s32[64]{0:T(128)} %param.30) | copy-start | bytes 772
  215.6 5.2 %copy-start.17 = (s32[64]{0:T(128)S(1)}, s32[64]{0:T(128)}, u32[]{:S(2)}) copy-start(s32[64]{0:T(128)} %param.31) | copy-start | bytes 772
  223.1 1.6 copy-start.3
  224.4 4.2 %copy-start.6 = (bf16[1024,2,1,128]{3,0,1,2:T(8,128)(2,1)}, bf16[1024,2,1,128]{3,0,1,2:T(8,128)(2,1)S(1)}, u32[]{:S(2)}) copy-start(bf16[1024,2,1,128]{3,0,1,2:T(8,128)(2,1)S(1)} %copy.228) | copy-start | bytes 1572868
  225.5 3.1 copy-start.8
  241.0 2.1 copy-start.9
  251.2 4.8 %copy-start.7 = (bf16[1024,2,1,128]{3,0,1,2:T(8,128)(2,1)S(1)}, bf16[1024,2,1,128]{3,0,1,2:T(8,128)(2,1)}, u32[]{:S(2)}) copy-start(bf16[1024,2,1,128]{3,0,1,2:T(8,128)(2,1)} %copy-done.6) | copy-start | bytes 1572868
  360.8 2.2 copy-start.4
  360.8 2.8 copy-start.5
  360.8 2.8 copy-start.18
  367.8 27.0 %copy-start.12 = (f32[512]{0:T(512)S(1)}, f32[512]{0:T(512)}, u32[]{:S(2)}) copy-start(f32[512]{0:T(512)} %param.25) | copy-start | bytes 6148
  394.8 3.4 copy-start.1
